TPU v7x, 512 devices: a whole 4x8x8 slice. The times are simulated.
512 devices in a mesh: pb: 16 (over y, x_lo), item: 32 (over x_hi, z, core).
Axes of the slice: x: 4 (x_hi: 2, x_lo: 2; x = x_hi * 2 + x_lo), y: 8, z: 8, core: 2. Of those that a mesh axis runs over, the one named last changes fastest.
Arguments:
- queries: bfloat16 [8192, 512], P(('pb', 'item')), may hold values from -2 to 2
- gate_query: bfloat16 [8192, 64], P(('pb', 'item')), may hold values from -6 to 250
- items: bfloat16 [16384, 512], P(('item', 'pb')), may hold values from -2 to 2
- gate_items: bfloat16 [16384, 64], P(('item', 'pb')), may hold values from -6 to 6
- slot_tiles: int32 [16, 192], P('pb', 'item'), may hold values from -1 to 15, as said below
- d_scores: bfloat16 [16, 192, 128, 128], P('pb', 'item'), may hold values from -6 to 6
Outputs:
- grad_queries: bfloat16 [8192, 512], P(('pb', 'item'))
- grad_gate_query: float32 [8192, 64], P(('pb', 'item'))
- grad_items: bfloat16 [16384, 512], P(('item', 'pb'))
- grad_gate_items: float32 [16384, 64], P(('item', 'pb'))
Inputs may be any that keep to these rules, and one draw needn't show every extreme that they name: `slot_tiles`: each device's row of slots names distinct tiles, live ones first and -1 after them. Devices (p, j) and (p, j + 32 / 2) form a pair: either one of them has all 6 slots live and the other exactly one, or both have between 1 and 3 live slots. Device (0, 0) has all 6 live.
All inputs are finite; a program needn't handle non-finite values.
Results may differ from a plain program's by a relative error of at most 0.0049.
Values may be sent and summed in bfloat16 or wider, within the bound.
No kernel may reach another device: no remote copies, remote signals or barrier semaphores. Data moves between devices by JAX's collectives and lax.ppermute only.
A program may use at most 64 MiB of HBM per device.

v0:
```python
import jax
import jax.numpy as jnp
from jax import lax
from jax.sharding import PartitionSpec as P

E = 64
KQ = 8
KI = 8


def tile_grads(query_tile, query_gate, item_tile, item_gate, cotangent):
    extent = query_tile.shape[0]
    query_parts = query_tile.reshape(extent, KQ, E)
    item_parts = item_tile.reshape(extent, KI, E)
    logits = jnp.einsum(
        "qae,ibe->abqi", query_parts, item_parts, preferred_element_type=jnp.float32
    ).reshape(KQ * KI, extent, extent)
    gates = (
        query_gate.astype(jnp.float32).T[:, :, None] + item_gate.astype(jnp.float32).T[:, None, :]
    )
    weights = jax.nn.softmax(gates, axis=0)
    score = jnp.sum(weights * logits, axis=0)
    upstream = cotangent.astype(jnp.float32)[None]
    logit_grad = (upstream * weights).astype(jnp.bfloat16)
    gate_grad = upstream * weights * (logits - score[None])
    logit_parts = logit_grad.reshape(KQ, KI, extent, extent)
    query_grad = jnp.einsum(
        "abqi,ibe->qae", logit_parts, item_parts, preferred_element_type=jnp.float32
    ).reshape(extent, KQ * E)
    item_grad = jnp.einsum(
        "abqi,qae->ibe", logit_parts, query_parts, preferred_element_type=jnp.float32
    ).reshape(extent, KI * E)
    return (query_grad, jnp.sum(gate_grad, axis=2).T, item_grad, jnp.sum(gate_grad, axis=1).T)


def on_device(queries, gate_query, items, gate_items, slot_tiles, d_scores):
    block_queries, block_gates = (
        lax.all_gather(queries, "item", axis=0, tiled=True),
        lax.all_gather(gate_query, "item", axis=0, tiled=True),
    )
    shard_items, shard_gates = (
        lax.all_gather(items, "pb", axis=0, tiled=True),
        lax.all_gather(gate_items, "pb", axis=0, tiled=True),
    )
    extent = d_scores.shape[-1]
    tile_ids = slot_tiles.reshape(-1)
    cotangents = d_scores.reshape(-1, extent, extent)
    slot_count = tile_ids.shape[0]
    item_blocks = shard_items.shape[0] // extent

    def anchors(tile_id):
        safe_id = jnp.maximum(tile_id, 0)
        return (safe_id // item_blocks * extent, safe_id % item_blocks * extent)

    def operands(tile_id):
        query_start, item_start = anchors(tile_id)
        return (
            lax.dynamic_slice_in_dim(block_queries, query_start, extent, 0),
            lax.dynamic_slice_in_dim(block_gates, query_start, extent, 0),
            lax.dynamic_slice_in_dim(shard_items, item_start, extent, 0),
            lax.dynamic_slice_in_dim(shard_gates, item_start, extent, 0),
        )

    def accumulate(current, tile_id, grads):
        query_start, item_start = anchors(tile_id)
        starts = (query_start, query_start, item_start, item_start)
        return tuple(
            (
                lax.dynamic_update_slice_in_dim(
                    total, lax.dynamic_slice_in_dim(total, start, extent, 0) + update, start, 0
                )
                for total, update, start in zip(current, grads, starts)
            )
        )

    totals = (
        jnp.zeros(block_queries.shape, jnp.float32),
        jnp.zeros(block_gates.shape, jnp.float32),
        jnp.zeros(shard_items.shape, jnp.float32),
        jnp.zeros(shard_gates.shape, jnp.float32),
    )

    def home_step(position, current):
        tile_id = tile_ids[position]

        def work(state):
            return accumulate(state, tile_id, tile_grads(*operands(tile_id), cotangents[position]))

        return lax.cond(tile_id >= 0, work, lambda state: state, current)

    totals = lax.fori_loop(0, slot_count, home_step, totals)
    query_sum, query_gate_sum = (
        lax.psum_scatter(totals[0], "item", scatter_dimension=0, tiled=True),
        lax.psum_scatter(totals[1], "item", scatter_dimension=0, tiled=True),
    )
    item_sum, item_gate_sum = (
        lax.psum_scatter(totals[2], "pb", scatter_dimension=0, tiled=True),
        lax.psum_scatter(totals[3], "pb", scatter_dimension=0, tiled=True),
    )
    return (
        query_sum.astype(jnp.bfloat16),
        query_gate_sum,
        item_sum.astype(jnp.bfloat16),
        item_gate_sum,
    )


def solution(mesh):
    return jax.shard_map(
        on_device,
        mesh=mesh,
        in_specs=(
            P(("pb", "item"), None),
            P(("pb", "item"), None),
            P(("item", "pb"), None),
            P(("item", "pb"), None),
            P("pb", "item"),
            P("pb", "item", None, None),
        ),
        out_specs=(
            P(("pb", "item"), None),
            P(("pb", "item"), None),
            P(("item", "pb"), None),
            P(("item", "pb"), None),
        ),
        check_vma=False,
    )
```

profile of v0, /device:TPU:4, one launch (start us, length us, event | category | flops | bytes accessed | tf_op | source)
XLA Modules:
  0.0 665.3 jit_solution(1207350731947987089)
XLA Ops:
  7.2 45.9 %all_gather.13 = bf16[512,64]{1,0:T(8,128)(2,1)S(1)} all-gather(bf16[16,64]{1,0:T(8,128)(2,1)} %param.11), channel_id=1, replica_groups=mesh['pb'=16,'item'=32] {'item'}, dimensions={0}, use_global_device_ids=true | all-gather | bytes 67584 | tf_op jit(solution)/shard_map/all_gather | solution.py:39
  53.2 0.1 copy.62
  53.3 35.4 %all_gather.14 = bf16[512,64]{1,0:T(8,128)(2,1)S(1)} all-gather(bf16[32,64]{1,0:T(8,128)(2,1)} %param.13), channel_id=1, replica_groups=mesh['pb'=16,'item'=32] {'pb'}, dimensions={0}, use_global_device_ids=true | all-gather | bytes 69632 | tf_op jit(solution)/shard_map/all_gather | solution.py:43
  88.7 0.7 copy.63
  89.4 1.7 copy.60
  91.2 38.1 %all_gather.15 = bf16[512,512]{1,0:T(8,128)(2,1)S(1)} all-gather(bf16[16,512]{1,0:T(8,128)(2,1)} %param.10), channel_id=1, replica_groups=mesh['pb'=16,'item'=32] {'item'}, dimensions={0}, use_global_device_ids=true | all-gather | bytes 540672 | tf_op jit(solution)/shard_map/all_gather | solution.py:38
  129.3 0.2 copy.64
  129.5 32.8 %all_gather.12 = bf16[512,512]{1,0:T(8,128)(2,1)S(1)} all-gather(bf16[32,512]{1,0:T(8,128)(2,1)} %param.12), channel_id=1, replica_groups=mesh['pb'=16,'item'=32] {'pb'}, dimensions={0}, use_global_device_ids=true | all-gather | bytes 557056 | tf_op jit(solution)/shard_map/all_gather | solution.py:42
  162.3 0.2 copy.61
  162.5 0.7 broadcast.34.clone
  163.1 0.7 broadcast.34
  163.8 0.1 broadcast.33.clone
  163.9 0.1 broadcast.33
  164.0 22.5 %while.19 = (s32[]{:T(128)}, f32[512,512]{0,1:T(8,128)S(1)}, f32[512,64]{0,1:T(8,128)}, f32[512,512]{0,1:T(8,128)S(1)}, f32[512,64]{0,1:T(8,128)}, /*index=5*/s3...) while((s32[]{:T(128)}, f32[512,512]{0,1:T(8,128)S(1)}, ...), condition=%wide.region_8.9_spmd, body=%wide.region_0.8_spmd.sunk | while | flops 432128032 | bytes 13894240 | solution.py:91
  164.1 0.6 dynamic_slice.46
  165.3 14.8 %conditional.2 = ((f32[512,512]{0,1:T(8,128)S(1)}, f32[512,64]{0,1:T(8,128)}, f32[512,512]{0,1:T(8,128)S(1)}, f32[512,64]{0,1:T(8,128)})) conditional(s32[]{:T(128)} %convert_element_type.27, (f32[512,512]{0,1:T(8,128)S(1)}, f32[512,64]{0,1:T(8,128)}, f32[512,512]{0,1:T(8,128)S(1)}, f32[512,64]{0,1:T(8,128)}) %tuple.50, (s32[]{:T(128)}, ...), branch_computations={%region_1.0_spmd, %region_2.7_spmd} | conditional | flops 432128032 | bytes 13893961 | solution.py:89
  166.0 0.8 bitcast_convert_fusion
  166.8 0.7 convert_bitcast_fusion
  167.5 1.2 add_reduce_fusion
  168.8 1.3 fusion.1
  170.0 0.1 copy.54
  170.1 0.1 copy.55
  170.3 1.3 fusion.7
  171.6 1.3 fusion.6
  173.0 0.1 constant_dynamic-update-slice_fusion
  173.0 0.1 constant_dynamic-update-slice_fusion.1
  173.1 1.3 fusion.2
  174.4 2.9 fusion.4
  177.4 1.4 fusion.8
  178.7 1.4 fusion.9
  180.1 0.6 dynamic_slice.46
  181.4 0.6 dynamic_slice.46
  182.7 0.6 dynamic_slice.46
  184.0 0.6 dynamic_slice.46
  185.2 0.6 dynamic_slice.46
  186.5 1.3 copy.65
  187.9 0.0 reduce-scatter.9.cloned.1.call-start
  187.9 1.4 copy.67
  189.3 0.0 reduce-scatter.7.cloned.1.call-start
  189.4 1.8 copy.66
  191.1 0.0 reduce-scatter.11.cloned.1.call-start
  191.2 1.7 copy.68
  193.0 188.1 %reduce-scatter.5.cloned.1.call-done = f32[16,512]{1,0:T(8,128)} async-done(((f32[512,512]{1,0:T(8,128)}), f32[16,512]{1,0:T(8,128)}) %reduce-scatter.5.cloned.1.call-update) | async-done | bytes 32784 | tf_op jit(solution)/shard_map/reduce_scatter | solution.py:93
  381.1 1.4 convert_element_type.21
  382.5 74.6 %reduce-scatter.9.cloned.1.call-done = f32[32,512]{1,0:T(8,128)} async-done(((f32[512,512]{1,0:T(8,128)}), f32[32,512]{1,0:T(8,128)}) %reduce-scatter.9.cloned.1.call-update) | async-done | bytes 65552 | tf_op jit(solution)/shard_map/reduce_scatter | solution.py:97
  457.1 1.5 convert_element_type.22
  458.6 125.6 %reduce-scatter.7.cloned.1.call-done = f32[16,64]{1,0:T(8,128)} async-done(((f32[512,64]{1,0:T(8,128)}), f32[16,64]{1,0:T(8,128)}) %reduce-scatter.7.cloned.1.call-update) | async-done | bytes 4112 | tf_op jit(solution)/shard_map/reduce_scatter | solution.py:94
  584.1 74.6 %reduce-scatter.11.cloned.1.call-done = f32[32,64]{1,0:T(8,128)} async-done(((f32[512,64]{1,0:T(8,128)}), f32[32,64]{1,0:T(8,128)}) %reduce-scatter.11.cloned.1.call-update) | async-done | bytes 8208 | tf_op jit(solution)/shard_map/reduce_scatter | solution.py:98
  (15 shorter events, 0.2 us)
Async XLA Ops:
  7.2 156.9 %copy-start = (s32[1,6]{1,0:T(1,128)S(1)}, s32[1,6]{1,0:T(1,128)}, u32[]{:S(2)}) copy-start(s32[1,6]{1,0:T(1,128)} %param.14) | copy-start | bytes 76
  7.2 373.9 %reduce-scatter.5.cloned.1.call-start = ((), (), s32[]{:S(2)}) async-start(), calls=%async_computation.4 | async-start | bytes 1081344 | tf_op jit(solution)/shard_map/reduce_scatter | solution.py:93
  187.9 269.2 %reduce-scatter.9.cloned.1.call-start = ((), (), s32[]{:S(2)}) async-start(), calls=%async_computation.6 | async-start | bytes 1114112 | tf_op jit(solution)/shard_map/reduce_scatter | solution.py:97
  189.3 394.8 %reduce-scatter.7.cloned.1.call-start = ((), (), s32[]{:S(2)}) async-start(), calls=%async_computation.5 | async-start | bytes 270336 | tf_op jit(solution)/shard_map/reduce_scatter | solution.py:94
  191.1 467.6 %reduce-scatter.11.cloned.1.call-start = ((), (), s32[]{:S(2)}) async-start(), calls=%async_computation.7 | async-start | bytes 278528 | tf_op jit(solution)/shard_map/reduce_scatter | solution.py:98
Sparse Core Ops, SparseCore 0:
  188.0 193.0 reduce-scatter.4
  383.9 73.1 reduce-scatter.8
  462.3 121.8 reduce-scatter.6
  587.4 71.3 reduce-scatter.10
where the time goes:
time: 667 us; the launch traced here: 665 us
  waiting for transfers between devices  463 us (69%)
  blocking collectives  152 us (23%)
  local copies, waits for them, and re-layouts  14.5 us (2%)
  between operations  13.8 us (2%)
  other arithmetic  12.6 us (2%)
    reduce_scatter x1, waiting for transfers between devices, on_device(): lax.psum_scatter(totals[0], 'item', scatter_dimension=0, tiled=True)  188 us
    reduce_scatter x1, waiting for transfers between devices, on_device(): lax.psum_scatter(totals[1], 'item', scatter_dimension=0, tiled=True)  126 us
    reduce_scatter x1, waiting for transfers between devices, on_device(): lax.psum_scatter(totals[2], 'pb', scatter_dimension=0, tiled=True)  74.6 us
    reduce_scatter x1, waiting for transfers between devices, on_device(): lax.psum_scatter(totals[3], 'pb', scatter_dimension=0, tiled=True)  74.6 us
    all_gather x1, blocking collectives, on_device(): lax.all_gather(gate_query, 'item', axis=0, tiled=True)  45.9 us
    all_gather x1, blocking collectives, on_device(): lax.all_gather(queries, 'item', axis=0, tiled=True)  38.1 us
    all_gather x1, blocking collectives, on_device(): lax.all_gather(gate_items, 'pb', axis=0, tiled=True)  35.4 us
    all_gather x1, blocking collectives, on_device(): lax.all_gather(items, 'pb', axis=0, tiled=True)  32.8 us
  transfers between devices with their start and end apart: 4, of which 4 were waited for; matrix products, arithmetic and copies ran while one was open for 1% of the time, Pallas kernels for 0%

commit v1 on v0

--- a/solution.py
+++ b/solution.py
@@ -40,7 +40,9 @@
     )
     shard_items, shard_gates = (
         lax.all_gather(items, "pb", axis=0, tiled=True),
-        lax.all_gather(gate_items, "pb", axis=0, tiled=True),
+        jnp.concatenate(
+            lax.all_to_all(jnp.stack([gate_items] * lax.axis_size("pb")), "pb", 0, 0), axis=0
+        ),
     )
     extent = d_scores.shape[-1]
     tile_ids = slot_tiles.reshape(-1)

time: 667 us -> 644 us (0.966)
  blocking collectives: 152 us -> 122 us
  starting transfers between devices: 0.16 us -> 8 us
    all_gather x1 -> x0, blocking collectives: 35.4 us -> none  [on_device(): lax.all_gather(gate_items, 'pb', axis=0, tiled=True)]
    all_gather x1, blocking collectives: 38.1 us -> 47.3 us  [on_device(): lax.all_gather(queries, 'item', axis=0, tiled=True)]
    all_gather x1, blocking collectives: 45.9 us -> 37 us  [on_device(): lax.all_gather(gate_query, 'item', axis=0, tiled=True)]
    all_to_all x0 -> x1, starting transfers between devices: none -> 7.84 us  [on_device(): lax.all_to_all(jnp.stack([gate_items] * lax.axis_size('pb')), 'pb', 0, 0)]
  transfers between devices with their start and end apart: 4 -> 5, of which waited for: 4 -> 4; matrix products, arithmetic and copies ran while one was open for 1% -> 2% of each run, Pallas kernels for 0% -> 0%
where the time goes in v1:
time: 644 us; the launch traced here: 642 us
  waiting for transfers between devices  461 us (72%)
  blocking collectives  122 us (19%)
  local copies, waits for them, and re-layouts  16.1 us (3%)
  between operations  13.8 us (2%)
  other arithmetic  12.6 us (2%)
  starting transfers between devices  8 us (1%)
    reduce_scatter x1, waiting for transfers between devices, on_device(): lax.psum_scatter(totals[0], 'item', scatter_dimension=0, tiled=True)  186 us
    reduce_scatter x1, waiting for transfers between devices, on_device(): lax.psum_scatter(totals[1], 'item', scatter_dimension=0, tiled=True)  125 us
    reduce_scatter x1, waiting for transfers between devices, on_device(): lax.psum_scatter(totals[2], 'pb', scatter_dimension=0, tiled=True)  74.5 us
    reduce_scatter x1, waiting for transfers between devices, on_device(): lax.psum_scatter(totals[3], 'pb', scatter_dimension=0, tiled=True)  74.4 us
    all_gather x1, blocking collectives, on_device(): lax.all_gather(queries, 'item', axis=0, tiled=True)  47.3 us
    all_gather x1, blocking collectives, on_device(): lax.all_gather(items, 'pb', axis=0, tiled=True)  37.7 us
    all_gather x1, blocking collectives, on_device(): lax.all_gather(gate_query, 'item', axis=0, tiled=True)  37 us
  transfers between devices with their start and end apart: 5, of which 4 were waited for; matrix products, arithmetic and copies ran while one was open for 2% of the time, Pallas kernels for 0%

profile of v1, /device:TPU:4, one launch (start us, length us, event | category | flops | bytes accessed | tf_op | source)
XLA Modules:
  0.0 642.3 jit_solution(5147280407762976191)
XLA Ops:
  7.2 0.7 stack.2
  7.9 0.8 reshape.69
  8.7 7.8 %all-to-all-start = ((bf16[16,2,1024]{2,1,0:T(2,128)(2,1)}), bf16[16,2,1024]{2,1,0:T(2,128)(2,1)S(1)}, u32[]{:S(2)}, u32[]{:S(2)}) async-start(bf16[16,2,1024]{2,1,0:T(2,128)(2,1)} %reshape.69), calls=%async_computation | async-start | bytes 131072 | tf_op jit(solution)/shard_map/all_to_all | solution.py:44
  16.5 47.3 %all_gather.11 = bf16[512,512]{1,0:T(8,128)(2,1)S(1)} all-gather(bf16[16,512]{1,0:T(8,128)(2,1)} %param.10), channel_id=1, replica_groups=mesh['pb'=16,'item'=32] {'item'}, dimensions={0}, use_global_device_ids=true | all-gather | bytes 540672 | tf_op jit(solution)/shard_map/all_gather | solution.py:38
  63.9 37.7 %all_gather.9 = bf16[512,512]{1,0:T(8,128)(2,1)S(1)} all-gather(bf16[32,512]{1,0:T(8,128)(2,1)} %param.12), channel_id=1, replica_groups=mesh['pb'=16,'item'=32] {'pb'}, dimensions={0}, use_global_device_ids=true | all-gather | bytes 557056 | tf_op jit(solution)/shard_map/all_gather | solution.py:42
  101.6 37.0 %all_gather.10 = bf16[512,64]{1,0:T(8,128)(2,1)S(1)} all-gather(bf16[16,64]{1,0:T(8,128)(2,1)} %param.11), channel_id=1, replica_groups=mesh['pb'=16,'item'=32] {'item'}, dimensions={0}, use_global_device_ids=true | all-gather | bytes 67584 | tf_op jit(solution)/shard_map/all_gather | solution.py:39
  138.7 0.1 copy.76
  138.8 1.7 copy.74
  140.5 0.2 copy.78
  140.7 0.2 copy.75
  140.9 0.1 reshape.70
  141.1 0.7 copy.77
  141.8 0.6 broadcast.36.clone
  142.5 0.7 broadcast.36
  143.1 0.1 broadcast.35.clone
  143.2 0.1 broadcast.35
  143.4 22.5 %while.19 = (s32[]{:T(128)}, f32[512,512]{0,1:T(8,128)S(1)}, f32[512,64]{0,1:T(8,128)}, f32[512,512]{0,1:T(8,128)S(1)}, f32[512,64]{0,1:T(8,128)}, /*index=5*/s3...) while((s32[]{:T(128)}, f32[512,512]{0,1:T(8,128)S(1)}, ...), condition=%wide.region_8.9_spmd, body=%wide.region_0.8_spmd.sunk | while | flops 432128032 | bytes 13894240 | solution.py:93
  143.4 0.6 dynamic_slice.46
  144.6 14.8 %conditional.2 = ((f32[512,512]{0,1:T(8,128)S(1)}, f32[512,64]{0,1:T(8,128)}, f32[512,512]{0,1:T(8,128)S(1)}, f32[512,64]{0,1:T(8,128)})) conditional(s32[]{:T(128)} %convert_element_type.27, (f32[512,512]{0,1:T(8,128)S(1)}, f32[512,64]{0,1:T(8,128)}, f32[512,512]{0,1:T(8,128)S(1)}, f32[512,64]{0,1:T(8,128)}) %tuple.51, (s32[]{:T(128)}, ...), branch_computations={%region_1.0_spmd, %region_2.7_spmd} | conditional | flops 432128032 | bytes 13893961 | solution.py:91
  145.3 0.8 bitcast_convert_fusion
  146.1 0.7 convert_bitcast_fusion
  146.8 1.2 add_reduce_fusion
  148.1 1.3 fusion.1
  149.4 0.1 copy.68
  149.5 0.1 copy.69
  149.6 1.3 fusion.7
  150.9 1.3 fusion.6
  152.3 0.1 constant_dynamic-update-slice_fusion
  152.4 0.1 constant_dynamic-update-slice_fusion.1
  152.5 1.3 fusion.2
  153.8 2.9 fusion.4
  156.7 1.4 fusion.8
  158.1 1.4 fusion.9
  159.5 0.6 dynamic_slice.46
  160.7 0.6 dynamic_slice.46
  162.0 0.6 dynamic_slice.46
  163.3 0.6 dynamic_slice.46
  164.6 0.6 dynamic_slice.46
  165.8 1.3 copy.79
  167.2 1.4 copy.81
  168.7 1.8 copy.80
  170.5 1.7 copy.82
  172.3 186.4 %reduce-scatter.5.cloned.1.call-done = f32[16,512]{1,0:T(8,128)} async-done(((f32[512,512]{1,0:T(8,128)}), f32[16,512]{1,0:T(8,128)}) %reduce-scatter.5.cloned.1.call-update) | async-done | bytes 32784 | tf_op jit(solution)/shard_map/reduce_scatter | solution.py:95
  358.7 1.4 convert_element_type.21
  360.1 74.5 %reduce-scatter.9.cloned.1.call-done = f32[32,512]{1,0:T(8,128)} async-done(((f32[512,512]{1,0:T(8,128)}), f32[32,512]{1,0:T(8,128)}) %reduce-scatter.9.cloned.1.call-update) | async-done | bytes 65552 | tf_op jit(solution)/shard_map/reduce_scatter | solution.py:99
  434.6 1.5 convert_element_type.22
  436.0 125.3 %reduce-scatter.7.cloned.1.call-done = f32[16,64]{1,0:T(8,128)} async-done(((f32[512,64]{1,0:T(8,128)}), f32[16,64]{1,0:T(8,128)}) %reduce-scatter.7.cloned.1.call-update) | async-done | bytes 4112 | tf_op jit(solution)/shard_map/reduce_scatter | solution.py:96
  561.3 74.4 %reduce-scatter.11.cloned.1.call-done = f32[32,64]{1,0:T(8,128)} async-done(((f32[512,64]{1,0:T(8,128)}), f32[32,64]{1,0:T(8,128)}) %reduce-scatter.11.cloned.1.call-update) | async-done | bytes 8208 | tf_op jit(solution)/shard_map/reduce_scatter | solution.py:100
  (19 shorter events, 0.4 us)
Async XLA Ops:
  7.2 136.2 %copy-start = (s32[1,6]{1,0:T(1,128)S(1)}, s32[1,6]{1,0:T(1,128)}, u32[]{:S(2)}) copy-start(s32[1,6]{1,0:T(1,128)} %param.14) | copy-start | bytes 76
  8.7 132.3 %all-to-all-start = ((bf16[16,2,1024]{2,1,0:T(2,128)(2,1)}), bf16[16,2,1024]{2,1,0:T(2,128)(2,1)S(1)}, u32[]{:S(2)}, u32[]{:S(2)}) async-start(bf16[16,2,1024]{2,1,0:T(2,128)(2,1)} %reshape.69), calls=%async_computation | async-start | bytes 131072 | tf_op jit(solution)/shard_map/all_to_all | solution.py:44
  16.5 342.2 %reduce-scatter.5.cloned.1.call-start = ((), (), s32[]{:S(2)}) async-start(), calls=%async_computation.5 | async-start | bytes 1081344 | tf_op jit(solution)/shard_map/reduce_scatter | solution.py:95
  167.2 267.4 %reduce-scatter.9.cloned.1.call-start = ((), (), s32[]{:S(2)}) async-start(), calls=%async_computation.7 | async-start | bytes 1114112 | tf_op jit(solution)/shard_map/reduce_scatter | solution.py:99
  168.6 392.7 %reduce-scatter.7.cloned.1.call-start = ((), (), s32[]{:S(2)}) async-start(), calls=%async_computation.6 | async-start | bytes 270336 | tf_op jit(solution)/shard_map/reduce_scatter | solution.py:96
  170.5 465.3 %reduce-scatter.11.cloned.1.call-start = ((), (), s32[]{:S(2)}) async-start(), calls=%async_computation.8 | async-start | bytes 278528 | tf_op jit(solution)/shard_map/reduce_scatter | solution.py:100
Sparse Core Ops, SparseCore 0:
  167.3 191.3 reduce-scatter.4
  361.5 73.0 reduce-scatter.8
  439.8 121.5 reduce-scatter.6
  564.6 71.1 reduce-scatter.10
